TPU v7x, 32 devices: a whole 2x2x4 slice. The times are simulated.
32 devices in a mesh: ka: 8 (over z, x), ga: 4 (over y, core).
Axes of the slice: x: 2, y: 2, z: 4, core: 2. Of those that a mesh axis runs over, the one named last changes fastest.
Arguments:
- coefficients: bfloat16 [8, 2, 256, 55296], P('ka', None, 'ga'), may hold values from -0.4375 to 0.4375
- shift_map: int32 [8, 3, 55296], P('ka', None, 'ga'), may hold values from 0 to 55295, as said below
- phase_angle: float32 [8, 3], P('ka'), may hold values from -3.140625 to 3.140625
Outputs:
- intersections: float32 [8, 3, 2, 256, 256], P('ka', None, None, 'ga')
Inputs may be any that keep to these rules, and one draw needn't show every extreme that they name: Each aligned block of 13824 consecutive entries of shift_map[k, b] is a permutation of the indices of that same block; it maps aligned tiles of 128 entries onto aligned tiles of 128 indices.
All inputs are finite; a program needn't handle non-finite values.
Results may differ from a plain program's by a relative error of at most 0.0003.
Values may be sent and summed in bfloat16 or wider, within the bound.
A program may use at most 192 MiB of HBM per device.

v0:
```python
import jax
import jax.numpy as jnp
from jax import lax
from jax.sharding import PartitionSpec as P


def passed_along(value, axis, steps):
    count = lax.axis_size(axis)
    pairs = [(source, (source + steps) % count) for source in range(count)]
    return lax.ppermute(value, axis, pairs)


def swapped(block, axis, bit):
    count = lax.axis_size(axis)
    route = []
    for low in range(count):
        high = low | 1 << bit
        if high != low and high < count:
            route += [(low, high), (high, low)]
    return lax.ppermute(block, axis, route)


def cross_terms(left, moved):
    prods = jnp.einsum("amg,bng->abmn", left, moved, preferred_element_type=jnp.float32)
    real_part = prods[0, 0] + prods[1, 1]
    imag_part = prods[0, 1] - prods[1, 0]
    return jnp.stack([real_part, imag_part])


def local(coefficients, shift_map, phase_angle):
    own = lax.all_to_all(coefficients, "ga", split_axis=3, concat_axis=2, tiled=True)
    next_x = passed_along(own, "ka", -4)
    next_y = swapped(own, "ka", 1)
    next_z = swapped(own, "ka", 0)
    block_width = own.shape[3]
    local_map = shift_map[0] - lax.axis_index("ga") * block_width
    left = own[0]
    movers = []
    for direction, other in enumerate((next_x, next_y, next_z)):
        movers.append(jnp.take(other[0], local_map[direction], axis=2))
    parts = jnp.stack([cross_terms(left, moved) for moved in movers])
    summed = lax.psum_scatter(
        jnp.transpose(parts, (2, 0, 1, 3)), "ga", scatter_dimension=0, tiled=True
    )
    summed = jnp.transpose(summed, (1, 2, 0, 3))
    real_part = summed[:, 0]
    imag_part = summed[:, 1]
    cosine = jnp.cos(phase_angle[0])[:, None, None]
    sine = jnp.sin(phase_angle[0])[:, None, None]
    rotated = jnp.stack(
        [cosine * real_part - sine * imag_part, sine * real_part + cosine * imag_part], axis=1
    )
    return rotated[None]


def solution(mesh):
    in_specs = (P("ka", None, "ga", None), P("ka", None, "ga"), P("ka", None))
    out_specs = P("ka", None, None, "ga", None)
    return jax.shard_map(local, mesh=mesh, in_specs=in_specs, out_specs=out_specs, check_vma=False)
```

profile of v0, /device:TPU:0, one launch (start us, length us, event | category | flops | bytes accessed | tf_op | source)
XLA Modules:
  0.0 1390.7 jit_solution(11480714659786665636)
XLA Ops:
  6.5 0.0 all-reduce.3.cloned.1.call-start
  6.5 56.5 %copy.60 = bf16[1,2,64,55296]{2,1,0,3:T(2,128)(2,1)} copy(bf16[1,2,64,55296]{3,2,1,0:T(8,128)(2,1)} %param.5) | data formatting | bytes 28311552 | tf_op args[0]
  63.0 41.2 %reshape.175 = bf16[4,2,884736]{2,1,0:T(2,128)(2,1)} reshape(bf16[55296,1,2,64]{3,2,1,0:T(2,128)(2,1)} %bitcast.81) | data formatting | bytes 28311552
  104.3 165.8 %all_to_all.18 = bf16[4,2,884736]{2,1,0:T(2,128)(2,1)} all-to-all(bf16[4,2,884736]{2,1,0:T(2,128)(2,1)} %reshape.175), channel_id=1, replica_groups=mesh['ka'=8,'ga'=4] {'ga'}, dimensions={0} | all-to-all | bytes 28311552 | tf_op jit(solution)/shard_map/all_to_all | solution.py:31
  270.1 40.5 %reshape.176 = bf16[55296,1,2,64]{3,2,1,0:T(2,128)(2,1)} reshape(bf16[4,2,884736]{2,1,0:T(2,128)(2,1)} %all_to_all.18) | data formatting | bytes 28311552
  310.6 68.9 %copy.80 = bf16[1,2,64,4,13824]{4,3,2,1,0:T(4,128)(2,1)} copy(bf16[1,2,64,4,13824]{2,1,4,3,0:T(2,128)(2,1)} %bitcast.80) | data formatting | bytes 28311552 | tf_op jit(solution)/shard_map/all_to_all | solution.py:31
  379.5 16.3 %copy.62 = bf16[1,2,4,64,13824]{4,3,2,1,0:T(8,128)(2,1)} copy(bf16[1,2,4,64,13824]{4,2,3,1,0:T(4,128)(2,1)} %bitcast.86) | data formatting | bytes 28311552 | tf_op jit(solution)/shard_map/all_to_all | solution.py:31
  395.8 0.0 copy-start
  395.8 34.6 %copy.63 = bf16[1,2,256,13824]{2,1,3,0:T(2,128)(2,1)} copy(bf16[1,2,256,13824]{3,2,1,0:T(8,128)(2,1)} %bitcast.82) | data formatting | bytes 28311552 | tf_op jit(solution)/shard_map/all_to_all | solution.py:31
  430.4 2.1 collective-permute-start.2
  432.5 2.6 collective-permute-start
  435.1 0.0 copy-done
  435.1 0.1 broadcast_subtract_fusion
  435.2 0.3 slice_reduce_fusion.2
  435.5 1.6 collective-permute-start.1
  437.4 299.1 %collective-permute-done.2 = bf16[1,2,256,13824]{2,1,3,0:T(2,128)(2,1)} collective-permute-done((bf16[1,2,256,13824]{2,1,3,0:T(2,128)(2,1)}, bf16[1,2,256,13824]{2,1,3,0:T(2,128)(2,1)}, u32[]{:S(2)}, u32[]{:S(2)}) %collective-permute-start.2) | collective-permute-done | bytes 14155808 | tf_op jit(solution)/shard_map/ppermute | solution.py:20
  736.5 55.4 %gather_fusion.2 = bf16[13824,2,256]{2,1,0:T(2,128)(2,1)} fusion(bf16[2,256,13824]{1,0,2:T(2,128)(2,1)} %bitcast.22, s32[14336]{0:T(1024)S(1)} %pad_clamp_fusion), kind=kCustom, calls=%fused_computation.2.clone | custom fusion | bytes 28366848 | tf_op jit(solution)/shard_map/jit(_take)/gather | solution.py:40
  791.9 52.0 %fusion.8 = bf16[2,256,13824]{1,0,2:T(2,128)(2,1)} fusion(bf16[13824,2,256]{2,1,0:T(2,128)(2,1)} %gather_fusion.2, pred[13824]{0:T(1024)(128)(4,1)S(1)} %compare_and_fusion), kind=kLoop, calls=%fused_computation.14 | loop fusion | flops 7077888 | bytes 28325376 | tf_op jit(solution)/shard_map/jit(_take)/select_n | solution.py:40
  843.9 34.9 %copy.72 = bf16[2,256,13824]{2,1,0:T(8,128)(2,1)} copy(bf16[2,256,13824]{1,0,2:T(2,128)(2,1)} %fusion.8) | data formatting | bytes 28311552 | tf_op jit(solution)/shard_map/jit(_take)/select_n | solution.py:40
  878.8 163.5 %collective-permute-done = bf16[1,2,256,13824]{2,1,3,0:T(2,128)(2,1)} collective-permute-done((bf16[1,2,256,13824]{2,1,3,0:T(2,128)(2,1)}, bf16[1,2,256,13824]{2,1,3,0:T(2,128)(2,1)}, u32[]{:S(2)}, u32[]{:S(2)}) %collective-permute-start) | collective-permute-done | bytes 14155808 | tf_op jit(solution)/shard_map/ppermute | solution.py:10
  1042.3 55.6 %gather_fusion = bf16[13824,2,256]{2,1,0:T(2,128)(2,1)} fusion(bf16[2,256,13824]{1,0,2:T(2,128)(2,1)} %bitcast.4, s32[14336]{0:T(1024)S(1)} %pad_clamp_fusion.2), kind=kCustom, calls=%fused_computation.clone | custom fusion | bytes 28366848 | tf_op jit(solution)/shard_map/jit(_take)/gather | solution.py:40
  1097.9 52.0 %fusion.6 = bf16[2,256,13824,1]{1,0,2,3:T(2,128)(2,1)} fusion(bf16[13824,2,256]{2,1,0:T(2,128)(2,1)} %gather_fusion, pred[13824]{0:T(1024)(128)(4,1)S(1)} %compare_and_fusion.2), kind=kLoop, calls=%fused_computation.12 | loop fusion | flops 7077888 | bytes 28325376 | tf_op jit(solution)/shard_map/jit(_take)/select_n | solution.py:40
  1150.0 14.8 %fusion.15 = f32[2,2,256,256]{2,3,0,1:T(8,128)S(1)} fusion(bf16[2,256,13824,1]{2,1,0,3:T(8,128)(2,1)} %bitcast.83, bf16[2,256,13824,1]{1,0,2,3:T(2,128)(2,1)} %fusion.6), kind=kOutput, calls=%fused_computation.18 | convolution fusion | flops 7247757312 | bytes 29360128 | tf_op jit(solution)/shard_map/amg,bng->abmn/dot_general | solution.py:24
  1164.8 14.8 %fusion.12 = f32[2,2,256,256]{2,3,1,0:T(8,128)S(1)} fusion(bf16[2,256,13824,1]{2,1,3,0:T(8,128)(2,1)} %bitcast.84, bf16[2,256,13824]{2,1,0:T(8,128)(2,1)} %copy.72), kind=kOutput, calls=%fused_computation.17 | convolution fusion | flops 7247757312 | bytes 29360128 | tf_op jit(solution)/shard_map/amg,bng->abmn/dot_general | solution.py:24
  1179.6 0.1 fusion.19
  1179.7 0.0 collective-permute-done.1
  1179.7 55.6 %gather_fusion.1 = bf16[13824,2,256]{2,1,0:T(2,128)(2,1)} fusion(bf16[2,256,13824]{1,0,2:T(2,128)(2,1)} %bitcast.13, s32[14336]{0:T(1024)S(1)} %pad_clamp_fusion.1), kind=kCustom, calls=%fused_computation.1.clone | custom fusion | bytes 28366848 | tf_op jit(solution)/shard_map/jit(_take)/gather | solution.py:40
  1235.3 52.0 %fusion.7 = bf16[2,256,13824]{1,0,2:T(2,128)(2,1)} fusion(bf16[13824,2,256]{2,1,0:T(2,128)(2,1)} %gather_fusion.1, pred[13824]{0:T(1024)(128)(4,1)S(1)} %compare_and_fusion.1), kind=kLoop, calls=%fused_computation.13 | loop fusion | flops 7077888 | bytes 28325376 | tf_op jit(solution)/shard_map/jit(_take)/select_n | solution.py:40
  1287.3 35.0 %copy.69 = bf16[2,256,13824]{2,1,0:T(8,128)(2,1)} copy(bf16[2,256,13824]{1,0,2:T(2,128)(2,1)} %fusion.7) | data formatting | bytes 28311552 | tf_op jit(solution)/shard_map/jit(_take)/select_n | solution.py:40
  1322.3 0.0 copy-start.2
  1322.3 0.0 copy-start.1
  1322.3 14.9 %fusion.9 = f32[2,2,256,256]{2,3,1,0:T(8,128)S(1)} fusion(bf16[2,256,13824,1]{2,1,3,0:T(8,128)(2,1)} %bitcast.85, bf16[2,256,13824]{2,1,0:T(8,128)(2,1)} %copy.69), kind=kOutput, calls=%fused_computation.16 | convolution fusion | flops 7247757312 | bytes 29360128 | tf_op jit(solution)/shard_map/amg,bng->abmn/dot_general | solution.py:24
  1337.2 0.1 fusion.21
  1337.3 0.1 maximum_bitcast_fusion.1
  1337.4 0.2 maximum_bitcast_fusion
  1337.6 2.1 copy.74
  1339.7 0.0 all-reduce.3.cloned.1.call-update
  1339.8 0.0 copy-done.2
  1339.8 0.6 dynamic-slice
  1341.0 0.0 copy-done.1
  1341.1 40.8 %all-reduce.3.cloned.1.call-done = f32[256,3,2,256]{3,2,1,0:T(2,128)} async-done(((f32[256,3,2,256]{3,2,1,0:T(2,128)}), f32[256,3,2,256]{3,2,1,0:T(2,128)}) %all-reduce.3.cloned.1.call-update) | async-done | bytes 1572880
  1381.9 1.1 constant_dynamic-slice_fusion
  1383.0 0.1 multiply_subtract_fusion
  1383.1 0.8 maximum_bitcast_fusion.4
  (14 shorter events, 0.3 us)
Async XLA Ops:
  6.5 1375.4 %all-reduce.3.cloned.1.call-start = ((), (), s32[]{:S(2)}) async-start(), calls=%async_computation.1 | async-start | bytes 3145728
  395.8 39.3 %copy-start = (s32[1,3,13824]{2,0,1:T(1,128)S(1)}, s32[1,3,13824]{2,0,1:T(1,128)}, u32[]{:S(2)}) copy-start(s32[1,3,13824]{2,0,1:T(1,128)} %param.6) | copy-start | bytes 497668
  430.4 306.1 %collective-permute-start.2 = (bf16[1,2,256,13824]{2,1,3,0:T(2,128)(2,1)}, bf16[1,2,256,13824]{2,1,3,0:T(2,128)(2,1)}, u32[]{:S(2)}, u32[]{:S(2)}) collective-permute-start(bf16[1,2,256,13824]{2,1,3,0:T(2,128)(2,1)} %copy.63), channel_id=1, source_target_pairs={{0,4},{4,0},{8,12},{12,8},{16,20},{20,16},{24,28},{28,24},{1,5},{5... | collective-permute-start | bytes 42467336 | tf_op jit(solution)/shard_map/ppermute | solution.py:20
  432.5 609.8 %collective-permute-start = (bf16[1,2,256,13824]{2,1,3,0:T(2,128)(2,1)}, bf16[1,2,256,13824]{2,1,3,0:T(2,128)(2,1)}, u32[]{:S(2)}, u32[]{:S(2)}) collective-permute-start(bf16[1,2,256,13824]{2,1,3,0:T(2,128)(2,1)} %copy.63), channel_id=1, source_target_pairs={{0,16},{4,20},{8,24},{12,28},{16,0},{20,4},{24,8},{28,12},{1,17},{... | collective-permute-start | bytes 42467336 | tf_op jit(solution)/shard_map/ppermute | solution.py:10
  435.5 744.2 %collective-permute-start.1 = (bf16[1,2,256,13824]{2,1,3,0:T(2,128)(2,1)}, bf16[1,2,256,13824]{2,1,3,0:T(2,128)(2,1)}, u32[]{:S(2)}, u32[]{:S(2)}) collective-permute-start(bf16[1,2,256,13824]{2,1,3,0:T(2,128)(2,1)} %copy.63), channel_id=1, source_target_pairs={{0,8},{8,0},{4,12},{12,4},{16,24},{24,16},{20,28},{28,20},{1,9},{9... | collective-permute-start | bytes 42467336 | tf_op jit(solution)/shard_map/ppermute | solution.py:20
  1322.3 17.5 %copy-start.2 = (u32[32]{0:T(128)S(1)}, u32[32]{0:T(128)}, u32[]{:S(2)}) copy-start(u32[32]{0:T(128)} %constant.21) | copy-start | bytes 388
  1322.3 18.7 %copy-start.1 = (f32[1,3]{1,0:T(1,128)S(1)}, f32[1,3]{1,0:T(1,128)}, u32[]{:S(2)}) copy-start(f32[1,3]{1,0:T(1,128)} %param.7) | copy-start | bytes 40
Sparse Core Ops, SparseCore 0:
  1339.9 41.9 all-reduce.2
where the time goes:
time: 1400 us; the launch traced here: 1390 us
  waiting for transfers between devices  503 us (36%)
  local copies, waits for them, and re-layouts  499 us (36%)
  blocking collectives  166 us (12%)
  other arithmetic  158 us (11%)
  matrix products  44.4 us (3%)
  between operations  14.3 us (1%)
    ppermute x2, waiting for transfers between devices, swapped(): return lax.ppermute(block, axis, route)  299 us
    gather x3, local copies, waits for them, and re-layouts, local(): movers.append(jnp.take(other[0], local_map[direction], axis=2))  167 us
    all_to_all x1, blocking collectives, local(): lax.all_to_all(coefficients, 'ga', split_axis=3, concat_axis=2, tiled=True)  166 us
    ppermute x1, waiting for transfers between devices, passed_along(): return lax.ppermute(value, axis, pairs)  163 us
    select_n x6, other arithmetic, local(): movers.append(jnp.take(other[0], local_map[direction], axis=2))  156 us
    unnamed x11, local copies, waits for them, and re-layouts  140 us
    all_to_all x3, local copies, waits for them, and re-layouts, local(): lax.all_to_all(coefficients, 'ga', split_axis=3, concat_axis=2, tiled=True)  120 us
    select_n x2, local copies, waits for them, and re-layouts, local(): movers.append(jnp.take(other[0], local_map[direction], axis=2))  69.9 us
  transfers between devices with their start and end apart: 4, of which 3 were waited for; matrix products, arithmetic and copies ran while one was open for 20% of the time, Pallas kernels for 0%

commit v1 on v0

--- a/solution.py
+++ b/solution.py
@@ -28,7 +28,9 @@
 
 
 def local(coefficients, shift_map, phase_angle):
-    own = lax.all_to_all(coefficients, "ga", split_axis=3, concat_axis=2, tiled=True)
+    own = jnp.concatenate(
+        lax.all_to_all(jnp.stack(jnp.split(coefficients, lax.psum(1, "ga"), 3), 0), "ga", 0, 0), 2
+    )
     next_x = passed_along(own, "ka", -4)
     next_y = swapped(own, "ka", 1)
     next_z = swapped(own, "ka", 0)

time: 1400 us -> 1180 us (0.84)
  local copies, waits for them, and re-layouts: 499 us -> 287 us
    unnamed x11 -> x8, local copies, waits for them, and re-layouts: 140 us -> 1.65 us
    all_to_all x3 -> x1, local copies, waits for them, and re-layouts: 120 us -> 6.38 us  [local(): lax.all_to_all(jnp.stack(jnp.split(coefficients, lax.psum(1, 'ga'), 3), 0...]
    reshape x0 -> x1, local copies, waits for them, and re-layouts: none -> 34.6 us  [local(): jnp.concatenate(lax.all_to_all(jnp.stack(jnp.split(coefficients, lax.psum...]
  transfers between devices with their start and end apart: 4 -> 4, of which waited for: 3 -> 3; matrix products, arithmetic and copies ran while one was open for 20% -> 24% of each run, Pallas kernels for 0% -> 0%
where the time goes in v1:
time: 1180 us
  waiting for transfers between devices  504 us (43%)
  local copies, waits for them, and re-layouts  287 us (24%)
  other arithmetic  161 us (14%)
  blocking collectives  159 us (13%)
  matrix products  44.5 us (4%)
  between operations  14.3 us (1%)
    ppermute x2, waiting for transfers between devices, swapped(): return lax.ppermute(block, axis, route)  299 us
    gather x3, local copies, waits for them, and re-layouts, local(): movers.append(jnp.take(other[0], local_map[direction], axis=2))  166 us
    ppermute x1, waiting for transfers between devices, passed_along(): return lax.ppermute(value, axis, pairs)  163 us
    all_to_all x1, blocking collectives, local(): lax.all_to_all(jnp.stack(jnp.split(coefficients, lax.psum(1, 'ga'), 3), 0...  159 us
    select_n x6, other arithmetic, local(): movers.append(jnp.take(other[0], local_map[direction], axis=2))  156 us
    select_n x2, local copies, waits for them, and re-layouts, local(): movers.append(jnp.take(other[0], local_map[direction], axis=2))  70 us
    dot_general x3, matrix products, cross_terms(): jnp.einsum('amg,bng->abmn', left, moved, preferred_element_type=jnp.float32)  44.5 us
    unnamed x2, waiting for transfers between devices  41.1 us
  transfers between devices with their start and end apart: 4, of which 3 were waited for; matrix products, arithmetic and copies ran while one was open for 24% of the time, Pallas kernels for 0%

profile of v1, /device:TPU:0, one launch (start us, length us, event | category | flops | bytes accessed | tf_op | source)
XLA Modules:
  0.0 1175.4 jit_solution(581700691758890815)
XLA Ops:
  6.5 0.0 all-reduce.3.cloned.1.call-start
  6.5 5.7 slice_bitcast_fusion.3
  12.2 3.2 pad_maximum_fusion
  15.4 158.9 %all_to_all.5 = bf16[4,1,2,64,13824]{4,3,2,1,0:T(8,128)(2,1)S(1)} all-to-all(bf16[4,1,2,64,13824]{4,3,2,1,0:T(8,128)(2,1)S(1)} %pad_maximum_fusion), channel_id=1, replica_groups=mesh['ka'=8,'ga'=4] {'ga'}, dimensions={0} | all-to-all | bytes 28311552 | tf_op jit(solution)/shard_map/all_to_all | solution.py:32
  174.3 6.4 copy.34
  180.7 0.0 copy-start
  180.7 34.6 %copy.35 = bf16[1,2,256,13824]{2,1,3,0:T(2,128)(2,1)} copy(bf16[1,2,256,13824]{3,2,1,0:T(8,128)(2,1)} %bitcast.87) | data formatting | bytes 28311552 | tf_op jit(solution)/shard_map/reshape | solution.py:31
  215.4 1.9 collective-permute-start.2
  217.3 2.6 collective-permute-start
  219.8 0.0 copy-done
  219.8 0.1 broadcast_subtract_fusion
  220.0 0.3 slice_reduce_fusion.2
  220.3 1.6 collective-permute-start.1
  222.1 299.1 %collective-permute-done.2 = bf16[1,2,256,13824]{2,1,3,0:T(2,128)(2,1)} collective-permute-done((bf16[1,2,256,13824]{2,1,3,0:T(2,128)(2,1)}, bf16[1,2,256,13824]{2,1,3,0:T(2,128)(2,1)}, u32[]{:S(2)}, u32[]{:S(2)}) %collective-permute-start.2) | collective-permute-done | bytes 14155808 | tf_op jit(solution)/shard_map/ppermute | solution.py:20
  521.2 55.4 %gather_fusion.2 = bf16[13824,2,256]{2,1,0:T(2,128)(2,1)} fusion(bf16[2,256,13824]{1,0,2:T(2,128)(2,1)} %bitcast.27, s32[14336]{0:T(1024)S(1)} %pad_clamp_fusion), kind=kCustom, calls=%fused_computation.2.clone | custom fusion | bytes 28366848 | tf_op jit(solution)/shard_map/jit(_take)/gather | solution.py:42
  576.6 52.0 %fusion.8 = bf16[2,256,13824]{1,0,2:T(2,128)(2,1)} fusion(bf16[13824,2,256]{2,1,0:T(2,128)(2,1)} %gather_fusion.2, pred[13824]{0:T(1024)(128)(4,1)S(1)} %compare_and_fusion), kind=kLoop, calls=%fused_computation.15 | loop fusion | flops 7077888 | bytes 28325376 | tf_op jit(solution)/shard_map/jit(_take)/select_n | solution.py:42
  628.7 35.0 %copy.43 = bf16[2,256,13824]{2,1,0:T(8,128)(2,1)} copy(bf16[2,256,13824]{1,0,2:T(2,128)(2,1)} %fusion.8) | data formatting | bytes 28311552 | tf_op jit(solution)/shard_map/jit(_take)/select_n | solution.py:42
  663.6 163.4 %collective-permute-done = bf16[1,2,256,13824]{2,1,3,0:T(2,128)(2,1)} collective-permute-done((bf16[1,2,256,13824]{2,1,3,0:T(2,128)(2,1)}, bf16[1,2,256,13824]{2,1,3,0:T(2,128)(2,1)}, u32[]{:S(2)}, u32[]{:S(2)}) %collective-permute-start) | collective-permute-done | bytes 14155808 | tf_op jit(solution)/shard_map/ppermute | solution.py:10
  827.1 55.4 %gather_fusion = bf16[13824,2,256]{2,1,0:T(2,128)(2,1)} fusion(bf16[2,256,13824]{1,0,2:T(2,128)(2,1)} %bitcast.7, s32[14336]{0:T(1024)S(1)} %pad_clamp_fusion.2), kind=kCustom, calls=%fused_computation.clone | custom fusion | bytes 28366848 | tf_op jit(solution)/shard_map/jit(_take)/gather | solution.py:42
  882.5 52.0 %fusion.6 = bf16[2,256,13824,1]{1,0,2,3:T(2,128)(2,1)} fusion(bf16[13824,2,256]{2,1,0:T(2,128)(2,1)} %gather_fusion, pred[13824]{0:T(1024)(128)(4,1)S(1)} %compare_and_fusion.2), kind=kLoop, calls=%fused_computation.13 | loop fusion | flops 7077888 | bytes 28325376 | tf_op jit(solution)/shard_map/jit(_take)/select_n | solution.py:42
  934.5 14.8 %fusion.15 = f32[2,2,256,256]{2,3,0,1:T(8,128)S(1)} fusion(bf16[2,256,13824,1]{2,1,0,3:T(8,128)(2,1)} %bitcast.88, bf16[2,256,13824,1]{1,0,2,3:T(2,128)(2,1)} %fusion.6), kind=kOutput, calls=%fused_computation.23 | convolution fusion | flops 7247757312 | bytes 29360128 | tf_op jit(solution)/shard_map/amg,bng->abmn/dot_general | solution.py:24
  949.4 14.8 %fusion.12 = f32[2,2,256,256]{2,3,1,0:T(8,128)S(1)} fusion(bf16[2,256,13824,1]{2,1,3,0:T(8,128)(2,1)} %bitcast.89, bf16[2,256,13824]{2,1,0:T(8,128)(2,1)} %copy.43), kind=kOutput, calls=%fused_computation.22 | convolution fusion | flops 7247757312 | bytes 29360128 | tf_op jit(solution)/shard_map/amg,bng->abmn/dot_general | solution.py:24
  964.2 0.1 fusion.19
  964.2 0.0 collective-permute-done.1
  964.3 55.4 %gather_fusion.1 = bf16[13824,2,256]{2,1,0:T(2,128)(2,1)} fusion(bf16[2,256,13824]{1,0,2:T(2,128)(2,1)} %bitcast.17, s32[14336]{0:T(1024)S(1)} %pad_clamp_fusion.1), kind=kCustom, calls=%fused_computation.1.clone | custom fusion | bytes 28366848 | tf_op jit(solution)/shard_map/jit(_take)/gather | solution.py:42
  1019.6 52.0 %fusion.7 = bf16[2,256,13824]{1,0,2:T(2,128)(2,1)} fusion(bf16[13824,2,256]{2,1,0:T(2,128)(2,1)} %gather_fusion.1, pred[13824]{0:T(1024)(128)(4,1)S(1)} %compare_and_fusion.1), kind=kLoop, calls=%fused_computation.14 | loop fusion | flops 7077888 | bytes 28325376 | tf_op jit(solution)/shard_map/jit(_take)/select_n | solution.py:42
  1071.6 35.0 %copy.40 = bf16[2,256,13824]{2,1,0:T(8,128)(2,1)} copy(bf16[2,256,13824]{1,0,2:T(2,128)(2,1)} %fusion.7) | data formatting | bytes 28311552 | tf_op jit(solution)/shard_map/jit(_take)/select_n | solution.py:42
  1106.6 0.0 copy-start.2
  1106.6 0.0 copy-start.1
  1106.6 14.9 %fusion.9 = f32[2,2,256,256]{2,3,1,0:T(8,128)S(1)} fusion(bf16[2,256,13824,1]{2,1,3,0:T(8,128)(2,1)} %bitcast.90, bf16[2,256,13824]{2,1,0:T(8,128)(2,1)} %copy.40), kind=kOutput, calls=%fused_computation.21 | convolution fusion | flops 7247757312 | bytes 29360128 | tf_op jit(solution)/shard_map/amg,bng->abmn/dot_general | solution.py:24
  1121.5 0.1 fusion.21
  1121.6 0.1 maximum_bitcast_fusion.1
  1121.7 0.2 maximum_bitcast_fusion
  1121.9 2.2 copy.45
  1124.1 0.0 all-reduce.3.cloned.1.call-update
  1124.1 0.0 copy-done.2
  1124.1 0.6 dynamic-slice
  1125.3 0.0 copy-done.1
  1125.4 41.1 %all-reduce.3.cloned.1.call-done = f32[256,3,2,256]{3,2,1,0:T(2,128)} async-done(((f32[256,3,2,256]{3,2,1,0:T(2,128)}), f32[256,3,2,256]{3,2,1,0:T(2,128)}) %all-reduce.3.cloned.1.call-update) | async-done | bytes 1572880
  1166.5 1.1 constant_dynamic-slice_fusion
  1167.6 0.1 multiply_subtract_fusion
  1167.7 0.8 maximum_bitcast_fusion.4
  (14 shorter events, 0.3 us)
Async XLA Ops:
  6.5 1160.0 %all-reduce.3.cloned.1.call-start = ((), (), s32[]{:S(2)}) async-start(), calls=%async_computation.1 | async-start | bytes 3145728
  180.7 39.1 %copy-start = (s32[1,3,13824]{2,0,1:T(1,128)S(1)}, s32[1,3,13824]{2,0,1:T(1,128)}, u32[]{:S(2)}) copy-start(s32[1,3,13824]{2,0,1:T(1,128)} %param.6) | copy-start | bytes 497668
  215.4 305.9 %collective-permute-start.2 = (bf16[1,2,256,13824]{2,1,3,0:T(2,128)(2,1)}, bf16[1,2,256,13824]{2,1,3,0:T(2,128)(2,1)}, u32[]{:S(2)}, u32[]{:S(2)}) collective-permute-start(bf16[1,2,256,13824]{2,1,3,0:T(2,128)(2,1)} %copy.35), channel_id=1, source_target_pairs={{0,4},{4,0},{8,12},{12,8},{16,20},{20,16},{24,28},{28,24},{1,5},{5... | collective-permute-start | bytes 42467336 | tf_op jit(solution)/shard_map/ppermute | solution.py:20
  217.3 609.8 %collective-permute-start = (bf16[1,2,256,13824]{2,1,3,0:T(2,128)(2,1)}, bf16[1,2,256,13824]{2,1,3,0:T(2,128)(2,1)}, u32[]{:S(2)}, u32[]{:S(2)}) collective-permute-start(bf16[1,2,256,13824]{2,1,3,0:T(2,128)(2,1)} %copy.35), channel_id=1, source_target_pairs={{0,16},{4,20},{8,24},{12,28},{16,0},{20,4},{24,8},{28,12},{1,17},{... | collective-permute-start | bytes 42467336 | tf_op jit(solution)/shard_map/ppermute | solution.py:10
  220.3 744.0 %collective-permute-start.1 = (bf16[1,2,256,13824]{2,1,3,0:T(2,128)(2,1)}, bf16[1,2,256,13824]{2,1,3,0:T(2,128)(2,1)}, u32[]{:S(2)}, u32[]{:S(2)}) collective-permute-start(bf16[1,2,256,13824]{2,1,3,0:T(2,128)(2,1)} %copy.35), channel_id=1, source_target_pairs={{0,8},{8,0},{4,12},{12,4},{16,24},{24,16},{20,28},{28,20},{1,9},{9... | collective-permute-start | bytes 42467336 | tf_op jit(solution)/shard_map/ppermute | solution.py:20
  1106.6 17.5 %copy-start.2 = (u32[32]{0:T(128)S(1)}, u32[32]{0:T(128)}, u32[]{:S(2)}) copy-start(u32[32]{0:T(128)} %constant.21) | copy-start | bytes 388
  1106.6 18.8 %copy-start.1 = (f32[1,3]{1,0:T(1,128)S(1)}, f32[1,3]{1,0:T(1,128)}, u32[]{:S(2)}) copy-start(f32[1,3]{1,0:T(1,128)} %param.7) | copy-start | bytes 40
Sparse Core Ops, SparseCore 0:
  1124.2 42.2 all-reduce.2
